TPU v7x, 512 devices: a whole 4x4x16 slice. The times are simulated.
512 devices in a mesh: tile: 16 (over x, y_hi, core), orient: 32 (over z, y_lo).
Axes of the slice: x: 4, y: 4 (y_hi: 2, y_lo: 2; y = y_hi * 2 + y_lo), z: 16, core: 2. Of those that a mesh axis runs over, the one named last changes fastest.
Arguments:
- micrograph: bfloat16 [4096, 512], P('tile'), may hold values from -140 to 140
- templates: bfloat16 [64, 384, 384], P('orient', 'tile'), may hold values from -6 to 6
- defocus: float32 [4], replicated, may hold values from 8 to 40
- group_of_tile: int32 [16], P('tile'), may hold values from 0 to 3
Outputs:
- top_score: float32 [4096, 128], P(('tile', 'orient'))
- zscore: float32 [4096, 128], P(('tile', 'orient'))
All inputs are finite; a program needn't handle non-finite values.
Results may differ from a plain program's by a relative error of at most 0.0085.
Values may be sent and summed in bfloat16 or wider, within the bound.
A program may use at most 64 MiB of HBM per device.

v0:
```python
import functools
import math

import jax
import jax.numpy as jnp
import numpy as np
from jax import lax
from jax.experimental import pallas as pl
from jax.experimental.pallas import tpu as pltpu
from jax.sharding import PartitionSpec as P

TS, STRIP, OUTC, LROW, LCOL = 384, 256, 128, 640, 512
KH = 336
KP = 384
BLK = 128
NQ = LCOL // BLK
CHIPS = 8
KC = KP // CHIPS
MESH = pl.DeviceIdType.MESH
BF, F32 = jnp.bfloat16, jnp.float32


def twiddle(rows, cols, modulus, sign):
    residue = np.arange(rows)[:, None] * np.arange(cols)[None, :] % modulus
    mirrored = modulus - residue
    angle = np.minimum(residue, mirrored).astype(np.float32) * np.float32(2 * math.pi / modulus)
    flipped = np.where(residue > mirrored, -1.0, 1.0).astype(np.float32)
    return np.cos(angle).astype(BF), (np.float32(sign) * flipped * np.sin(angle)).astype(BF)


def tables():
    cc, cs = twiddle(LCOL, LCOL, LCOL, -1.0)
    col = np.stack(
        [
            np.concatenate([cc[:, q * BLK : (q + 1) * BLK], cs[:, q * BLK : (q + 1) * BLK]], 1)
            for q in range(NQ)
        ]
    )
    col_sum = col[:, :TS].astype(np.float32).sum(1, keepdims=True)
    rc, rs = twiddle(LROW, LROW, LROW, -1.0)
    rows = np.zeros((2 * KH, LROW), BF)
    half = LROW // 2 + 1
    rows[:half], rows[KH : KH + half] = rc[:half], rs[:half]
    bc, bs = twiddle(LCOL, OUTC, LCOL, 1.0)
    back = np.concatenate(
        [
            np.block(
                [
                    [bc[q * BLK : (q + 1) * BLK], bs[q * BLK : (q + 1) * BLK]],
                    [-bs[q * BLK : (q + 1) * BLK], bc[q * BLK : (q + 1) * BLK]],
                ]
            )
            for q in range(NQ)
        ]
    ).astype(BF)
    ac, as_ = twiddle(STRIP, LROW, LROW, 1.0)
    weight = np.full(half, 2.0, np.float32)
    weight[0] = weight[-1] = 1.0
    out = np.zeros((STRIP, 2 * KH), np.float32)
    out[:, :half] = weight * ac[:, :half].astype(np.float32)
    out[:, KH : KH + half] = -weight * as_[:, :half].astype(np.float32)
    return rows, col, back, out.astype(BF), col_sum


def combine(product, n=KH):
    real = product[:n, :BLK] - product[n:, BLK:]
    imag = product[:n, BLK:] + product[n:, :BLK]
    return real, imag


def kernel(
    mic, tpl, defo, group, rows_h, col_h, back_h, out_h, col_sum,
    top_o, z_o,
    rows, col, back, outt, frame, cspec, spec, ybuf, tg, tr, tf, tspec, hsp,
    psend, pown, precv, comb, rsb, gall, ctf_s, ctf_c, qb, ys, sbuf, rbuf,
    lsem, ssem, rsem, asem, bsem,
):
    t, o = lax.axis_index("tile"), lax.axis_index("orient")
    z, ylo = o // 2, o % 2
    j, c = t // 2, t % 2
    x, yh = j // 2, j % 2
    other = 1 - c

    def orient_at(tile):
        return z * 2 + (ylo + yh + (tile // 2) % 2) % 2

    def near(tile):
        return (tile, orient_at(tile))

    loads = [
        pltpu.make_async_copy(mic, frame.at[pl.ds(0, STRIP)], lsem.at[0]),
        pltpu.make_async_copy(col_h, col, lsem.at[1]),
        pltpu.make_async_copy(rows_h, rows, lsem.at[2]),
        pltpu.make_async_copy(back_h, back, lsem.at[3]),
        pltpu.make_async_copy(out_h, outt, lsem.at[4]),
        pltpu.make_async_copy(tpl.at[c], tg.at[t], lsem.at[5]),
    ]
    for copy in loads:
        copy.start()

    barrier = pltpu.get_barrier_semaphore()

    def greet(device):
        pl.semaphore_signal(barrier, inc=1, device_id=device, device_id_type=MESH)

    def orient_peer(d):
        return (t, lax.rem(o + d, 32))

    def greet_orient(d, carry):
        greet(orient_peer(d))
        return carry

    for d in (1, 2, 14, 15):
        greet(near(lax.rem(t + d, 16)))
    ty = x * 4 + (1 - yh) * 2 + c
    greet((ty, o))
    partner = (j * 2 + other, o)
    greet(partner)
    for dx in (1, 2, 3):
        for core in (0, 1):
            greet((lax.rem(x + dx, 4) * 4 + yh * 2 + core, o))
    for d in range(1, CHIPS):
        greet(near(lax.rem(j + d, CHIPS) * 2 + c))
    lax.fori_loop(1, 32, greet_orient, 0)

    started = []

    def remote(src, dst, send, recv, device):
        return pltpu.make_async_remote_copy(
            src_ref=src, dst_ref=dst, send_sem=send, recv_sem=recv, device_id=device, device_id_type=MESH
        )

    def send(src, dst, index, recv_index, device):
        copy = remote(src, dst, ssem.at[index], rsem.at[recv_index], device)
        copy.start()
        started.append(copy)

    def arrive(dst, index):
        remote(dst, dst, ssem.at[0], rsem.at[index], partner).wait_recv()

    loads[0].wait()
    loads[1].wait()
    for q in range(NQ):
        cspec[q, 0:STRIP, :] = jnp.dot(
            frame[0:STRIP, :], col[q], preferred_element_type=F32
        ).astype(BF)

    pl.semaphore_wait(barrier, 4 + 1 + 1 + 6 + 7 + 31)

    t1, t2 = lax.rem(t + 15, 16), lax.rem(t + 14, 16)
    send(mic, frame.at[pl.ds(STRIP, STRIP)], 0, 0, near(t1))
    send(mic.at[pl.ds(0, BLK)], frame.at[pl.ds(2 * STRIP, BLK)], 1, 1, near(t2))
    send(tpl, ybuf, 2, 2, (ty, o))

    chosen = group[0]
    depth = jnp.float32(0.0)
    for g in range(4):
        depth = depth + jnp.where(chosen == g, defo[g], 0.0)
    depth = depth * jnp.float32(math.pi)
    k = lax.broadcasted_iota(jnp.int32, (KH, BLK), 0).astype(F32) / LROW
    angle = depth * (k * k) + 0.07
    ctf_s[...] = jnp.sin(angle)
    ctf_c[...] = jnp.cos(angle)

    arrive(ybuf, 2)
    fill = pltpu.make_async_copy(ybuf.at[c], tg.at[ty], lsem.at[6])
    fill.start()
    at = 3
    for dx in (1, 2, 3):
        xd = lax.rem(x + dx, 4)
        for core in (0, 1):
            for piece in (0, 1):
                src = tpl.at[core] if piece == 0 else ybuf.at[core]
                slot = t if piece == 0 else ty
                send(
                    src, tg.at[slot], at, 3 + (dx - 1) * 4 + c * 2 + piece,
                    (xd * 4 + yh * 2 + core, o),
                )
                at += 1
    send(tpl.at[other], tg.at[t], 15, 15, partner)
    send(ybuf.at[other], tg.at[ty], 16, 16, partner)

    arrive(frame.at[pl.ds(STRIP, STRIP)], 0)
    arrive(frame.at[pl.ds(2 * STRIP, BLK)], 1)
    keep1 = jnp.where(t < 15, 1.0, 0.0).astype(F32)
    keep2 = jnp.where(t < 14, 1.0, 0.0).astype(F32)
    row = lax.broadcasted_iota(jnp.int32, (TS, 2 * BLK), 0)
    keep = jnp.where(row < STRIP, keep1, keep2)
    for q in range(NQ):
        part = jnp.dot(frame[STRIP:LROW, :], col[q], preferred_element_type=F32)
        cspec[q, STRIP:LROW, :] = (part * keep).astype(BF)
    loads[2].wait()

    def spectrum(q):
        real, imag = combine(jnp.dot(rows[...], cspec[q], preferred_element_type=F32))
        spec[q, :, 0:BLK] = real
        spec[q, :, BLK:] = imag
        return real * real + imag * imag

    for i in range(2):
        psend[i] = spectrum(2 * other + i).astype(BF)
    send(psend, precv, 17, 17, partner)
    for i in range(2):
        pown[i, 0:KH, :] = spectrum(2 * c + i)
        pown[i, KH:KP, :] = jnp.zeros((KP - KH, BLK), F32)

    for dx in (1, 2, 3):
        xs = lax.rem(x + 4 - dx, 4)
        for core in (0, 1):
            for piece in (0, 1):
                row_of = yh if piece == 0 else 1 - yh
                arrive(tg.at[xs * 4 + row_of * 2 + core], 3 + (dx - 1) * 4 + core * 2 + piece)
    arrive(tg.at[j * 2 + other], 15)
    arrive(tg.at[x * 4 + (1 - yh) * 2 + other], 16)
    loads[5].wait()
    fill.wait()
    send(tg, tr, 18, 18, partner)

    arrive(precv, 17)
    for i in range(2):
        pown[i, 0:KH, :] = pown[i, 0:KH, :] + precv[i].astype(F32)
        for n in range(CHIPS):
            comb[n, i] = pown[i, n * KC : (n + 1) * KC, :].astype(BF)
    for d in range(1, CHIPS):
        to = lax.rem(j + d, CHIPS)
        send(comb.at[to], rsb.at[d - 1], 18 + d, 18 + d, near(to * 2 + c))

    arrive(tr, 18)
    for n, held in enumerate((tg, tr)):
        for s in range(16):
            tf[s * 24 : (s + 1) * 24, :] = held[s].astype(F32)
        values = tf[...]
        mean = jnp.sum(values) / (TS * TS)
        spread = jnp.sum(values * values) / (TS * TS) - mean * mean + 1e-05
        inverse = lax.rsqrt(jnp.full((1, 2 * BLK), spread, F32)) / (LROW * LCOL)
        rounded = values.astype(BF)
        for q in range(NQ):
            part = jnp.dot(rounded, col[q, 0:TS, :], preferred_element_type=F32)
            tspec[n, q] = ((part - mean * col_sum[q]) * inverse).astype(BF)

    for d in range(1, CHIPS):
        arrive(rsb.at[d - 1], 18 + d)
    total = comb[j].astype(F32)
    for d in range(1, CHIPS):
        total = total + rsb[d - 1].astype(F32)
    gall[c, j] = total.astype(BF)
    for d in range(1, CHIPS):
        to = lax.rem(j + d, CHIPS)
        send(gall.at[c, j], gall.at[c, j], 25 + d, 25 + d, near(to * 2 + c))

    for n in range(2):
        for q in range(NQ):
            real, imag = combine(
                jnp.dot(rows[:, 0:TS], tspec[n, q], preferred_element_type=F32)
            )
            hsp[n, q, :, 0:BLK] = real
            hsp[n, q, :, BLK:] = imag

    for d in range(1, CHIPS):
        arrive(gall.at[c, lax.rem(j + CHIPS - d, CHIPS)], 25 + d)
    send(gall.at[c], gall.at[c], 33, 33, partner)
    arrive(gall.at[other], 33)

    def power(q):
        return jnp.concatenate([gall[q // 2, n, q % 2].astype(F32) for n in range(CHIPS)], 0)

    k = lax.broadcasted_iota(jnp.int32, (KP, BLK), 0)
    weight = jnp.where(k < LROW // 2, 2.0, 1.0) * jnp.where(k <= LROW // 2, 1.0, 0.0)
    weight = jnp.where(k == 0, 1.0, weight)
    summed = jnp.zeros((KP, BLK), F32)
    for q in range(NQ):
        summed = summed + power(q)
    average = jnp.sum(summed * weight) / (LROW * LCOL * 16.0)
    for q in range(NQ):
        lane = lax.broadcasted_iota(jnp.int32, (1, BLK), 1) + q * BLK
        lane = jnp.where(2 * lane < LCOL, lane, lane - LCOL).astype(F32) / LCOL
        phase = depth * (lane * lane)
        factor = -(ctf_s[...] * jnp.cos(phase) + ctf_c[...] * jnp.sin(phase))
        factor = factor * lax.rsqrt(power(q)[0:KH] / 16.0 + average)
        real, imag = spec[q, :, 0:BLK] * factor, spec[q, :, BLK:] * factor
        for n in range(2):
            h_re, h_im = hsp[n, q, :, 0:BLK], hsp[n, q, :, BLK:]
            qb[n * KH : (n + 1) * KH, q * 256 : q * 256 + BLK] = (real * h_re + imag * h_im).astype(BF)
            qb[n * KH : (n + 1) * KH, q * 256 + BLK : (q + 1) * 256] = (imag * h_re - real * h_im).astype(BF)
    loads[3].wait()
    loads[4].wait()
    for n in range(2):
        y = jnp.dot(
            qb[n * KH : (n + 1) * KH, :], back[...], preferred_element_type=F32
        ).astype(BF)
        ys[0:KH, n * BLK : (n + 1) * BLK] = y[:, 0:BLK]
        ys[KH:, n * BLK : (n + 1) * BLK] = y[:, BLK:]
    score = jnp.dot(outt[...], ys[...], preferred_element_type=F32)
    for n in range(32):
        block = score[n * 8 : (n + 1) * 8, :]
        sbuf[n] = jnp.concatenate([block[:, 0:BLK], block[:, BLK:]], 0).astype(BF)

    def a2a(d):
        to = lax.rem(o + d, 32)
        return remote(sbuf.at[to], rbuf.at[o], asem.at[d], bsem.at[d], (t, to))

    def a2a_start(d, carry):
        a2a(d).start()
        return carry

    def a2a_wait(d, carry):
        src = lax.rem(o + 32 - d, 32)
        remote(rbuf.at[src], rbuf.at[src], asem.at[d], bsem.at[d], partner).wait_recv()
        return carry

    def a2a_sent(d, carry):
        a2a(d).wait_send()
        return carry

    lax.fori_loop(1, 32, a2a_start, 0)
    keep_own = pltpu.make_async_copy(sbuf.at[o], rbuf.at[o], lsem.at[7])
    keep_own.start()
    for copy in started:
        copy.wait_send()
    keep_own.wait()
    lax.fori_loop(1, 32, a2a_wait, 0)
    best = jnp.full((8, BLK), -jnp.inf, F32)
    first = jnp.zeros((8, BLK), F32)
    second = jnp.zeros((8, BLK), F32)
    for n in range(32):
        pair = rbuf[n].astype(F32)
        a, b = pair[0:8], pair[8:16]
        best = jnp.maximum(best, jnp.maximum(a, b))
        first = first + (a + b)
        second = second + (a * a + b * b)
    mean = first / 64.0
    spread = second / 64.0 - mean * mean
    top_o[...] = best
    z_o[...] = (best - mean) / jnp.sqrt(spread + 1e-05)
    lax.fori_loop(1, 32, a2a_sent, 0)


def local(consts, micrograph, templates, defocus, group_of_tile):
    rows, col, back, out, col_sum = consts
    hbm = pl.BlockSpec(memory_space=pl.ANY)
    vmem = pl.BlockSpec(memory_space=pltpu.VMEM)
    smem = pl.BlockSpec(memory_space=pltpu.SMEM)
    v = pltpu.VMEM
    return pl.pallas_call(
        kernel,
        out_shape=(jax.ShapeDtypeStruct((8, OUTC), F32),) * 2,
        in_specs=[hbm, hbm, smem, smem, hbm, hbm, hbm, hbm, vmem],
        out_specs=(vmem, vmem),
        scratch_shapes=[
            v((2 * KH, LROW), BF),
            v((NQ, LCOL, 2 * BLK), BF),
            v((2 * LCOL, 2 * OUTC), BF),
            v((STRIP, 2 * KH), BF),
            v((LROW, LCOL), BF),
            v((NQ, LROW, 2 * BLK), BF),
            v((NQ, KH, 2 * BLK), F32),
            v((2, 24, TS), BF),
            v((16, 24, TS), BF),
            v((16, 24, TS), BF),
            v((TS, TS), F32),
            v((2, NQ, TS, 2 * BLK), BF),
            v((2, NQ, KH, 2 * BLK), F32),
            v((2, KH, BLK), BF),
            v((2, KP, BLK), F32),
            v((2, KH, BLK), BF),
            v((CHIPS, 2, KC, BLK), BF),
            v((CHIPS - 1, 2, KC, BLK), BF),
            v((2, CHIPS, 2, KC, BLK), BF),
            v((KH, BLK), F32),
            v((KH, BLK), F32),
            v((2 * KH, 2 * LCOL), BF),
            v((2 * KH, 2 * BLK), BF),
            v((32, 16, BLK), BF),
            v((32, 16, BLK), BF),
            pltpu.SemaphoreType.DMA((8,)),
            pltpu.SemaphoreType.DMA((34,)),
            pltpu.SemaphoreType.DMA((34,)),
            pltpu.SemaphoreType.DMA((32,)),
            pltpu.SemaphoreType.DMA((32,)),
        ],
        compiler_params=pltpu.CompilerParams(collective_id=0, has_side_effects=True),
        name="match",
    )(micrograph, templates, defocus, group_of_tile, rows, col, back, out, col_sum)


def solution(mesh):
    consts = tuple(jnp.asarray(a) for a in tables())
    return jax.shard_map(
        functools.partial(local, consts),
        mesh=mesh,
        in_specs=(P("tile", None), P("orient", "tile", None), P(), P("tile")),
        out_specs=(P(("tile", "orient"), None),) * 2,
        check_vma=False,
    )
```

profile of v0, /device:TPU:1, one launch (start us, length us, event | category | flops | bytes accessed | tf_op | source)
XLA Modules:
  0.0 58.5 jit_solution(2371058144589627370)
XLA Ops:
  1.3 55.3 %match.1 = (f32[8,128]{1,0:T(8,128)}, f32[8,128]{1,0:T(8,128)}) custom-call(bf16[256,512]{1,0:T(8,128)(2,1)} %mic.1, bf16[2,24,384]{2,1,0:T(8,128)(2,1)} %tpl.1, f32[4]{0:T(128)} %defo.1, s32[1]{0:T(128)S(6)} %copy.13.group, bf16[672,640]{1,0:T(8,128)(2,1)} %constant.10.clone.rows_h, bf16[4,512,256]{2,1,0:T(8,128)(2,1)} %constant.11.clone.col_h, ...), custom_call_target="tpu_custom_call" | custom-call | tf_op jit(solution)/shard_map/match/pallas_call | solution.py:344
  56.6 0.0 copy-start
  56.6 1.3 %copy.14 = f32[8,128]{1,0:T(8,128)} copy(f32[8,128]{1,0:T(8,128)} %get-tuple-element.4) | data formatting | bytes 8192
  57.9 0.0 copy-done
  57.9 0.6 %copy.15 = f32[8,128]{1,0:T(8,128)} copy(f32[8,128]{1,0:T(8,128)S(1)} %copy-done) | data formatting | bytes 8192
Async XLA Ops:
  56.6 1.3 %copy-start = (f32[8,128]{1,0:T(8,128)S(1)}, f32[8,128]{1,0:T(8,128)}, u32[]{:S(2)}) copy-start(f32[8,128]{1,0:T(8,128)} %get-tuple-element.5) | copy-start | bytes 12292
where the time goes:
time: 58.7 us; the launch traced here: 58.5 us
  Pallas kernels  55.3 us (94%)
  local copies, waits for them, and re-layouts  1.86 us (3%)
  between operations  1.29 us (2%)
    pallas_call x1, Pallas kernels, local(): pl.pallas_call(kernel, out_shape=(jax.ShapeDtypeStruct((8, OUTC), F32),)...  55.3 us
    unnamed x4, local copies, waits for them, and re-layouts  1.86 us

commit v1 on v0

--- a/solution.py
+++ b/solution.py
@@ -16,6 +16,7 @@
 NQ = LCOL // BLK
 CHIPS = 8
 KC = KP // CHIPS
+FAR_FIRST = (3, 5, 4, 2, 6, 1, 7)
 MESH = pl.DeviceIdType.MESH
 BF, F32 = jnp.bfloat16, jnp.float32
 
@@ -70,10 +71,10 @@
 
 def kernel(
     mic, tpl, defo, group, rows_h, col_h, back_h, out_h, col_sum,
-    top_o, z_o,
+    res_o,
     rows, col, back, outt, frame, cspec, spec, ybuf, tg, tr, tf, tspec, hsp,
     psend, pown, precv, comb, rsb, gall, ctf_s, ctf_c, qb, ys, sbuf, rbuf,
-    lsem, ssem, rsem, asem, bsem,
+    lsem, ssem, rsem, asem, bsem, esem,
 ):
     t, o = lax.axis_index("tile"), lax.axis_index("orient")
     z, ylo = o // 2, o % 2
@@ -106,12 +107,10 @@
     def orient_peer(d):
         return (t, lax.rem(o + d, 32))
 
-    def greet_orient(d, carry):
+    beside = near(lax.rem(j + CHIPS + 2 * c - 1, CHIPS) * 2 + other)
+    greet(beside)
+    for d in (1, 31):
         greet(orient_peer(d))
-        return carry
-
-    for d in (1, 2, 14, 15):
-        greet(near(lax.rem(t + d, 16)))
     ty = x * 4 + (1 - yh) * 2 + c
     greet((ty, o))
     partner = (j * 2 + other, o)
@@ -121,7 +120,6 @@
             greet((lax.rem(x + dx, 4) * 4 + yh * 2 + core, o))
     for d in range(1, CHIPS):
         greet(near(lax.rem(j + d, CHIPS) * 2 + c))
-    lax.fori_loop(1, 32, greet_orient, 0)
 
     started = []
 
@@ -138,19 +136,47 @@
     def arrive(dst, index):
         remote(dst, dst, ssem.at[0], rsem.at[index], partner).wait_recv()
 
+    def tell(r):
+        step = max(1, 2 ** (r - 1))
+        for d in (step, 32 - step):
+            pl.semaphore_signal(
+                esem.at[r - 1], inc=1, device_id=orient_peer(d), device_id_type=MESH
+            )
+
+    def told(r):
+        pl.semaphore_wait(esem.at[r - 1], 2)
+
+    pl.semaphore_wait(barrier, 1 + 2 + 1 + 1 + 6 + 7)
+
+    before = lax.rem(j + CHIPS - 1, CHIPS)
+    across = near(before * 2 + 1)
+    last = c == 1
+    first_rows, second_rows = mic.at[pl.ds(0, BLK)], mic.at[pl.ds(BLK, BLK)]
+    send(
+        first_rows, frame.at[pl.ds(pl.multiple_of(STRIP + STRIP * c, STRIP), BLK)],
+        0, 35 + 2 * c, across,
+    )
+    there = (jnp.where(last, j, before) * 2 + other, jnp.where(last, o, across[1]))
+    send(second_rows, frame.at[pl.ds(STRIP + BLK, BLK)], 1, 36, there)
+    inner = [
+        remote(first_rows, frame.at[pl.ds(STRIP, BLK)], ssem.at[34], rsem.at[35], partner),
+        remote(
+            frame.at[pl.ds(STRIP, BLK)], frame.at[pl.ds(2 * STRIP, BLK)], ssem.at[35], rsem.at[37], partner
+        ),
+    ]
+
+    @pl.when(last)
+    def _():
+        inner[0].start()
+
+    send(tpl, ybuf, 2, 2, (ty, o))
+    tell(1)
     loads[0].wait()
     loads[1].wait()
     for q in range(NQ):
         cspec[q, 0:STRIP, :] = jnp.dot(
             frame[0:STRIP, :], col[q], preferred_element_type=F32
         ).astype(BF)
-
-    pl.semaphore_wait(barrier, 4 + 1 + 1 + 6 + 7 + 31)
-
-    t1, t2 = lax.rem(t + 15, 16), lax.rem(t + 14, 16)
-    send(mic, frame.at[pl.ds(STRIP, STRIP)], 0, 0, near(t1))
-    send(mic.at[pl.ds(0, BLK)], frame.at[pl.ds(2 * STRIP, BLK)], 1, 1, near(t2))
-    send(tpl, ybuf, 2, 2, (ty, o))
 
     chosen = group[0]
     depth = jnp.float32(0.0)
@@ -180,8 +206,16 @@
     send(tpl.at[other], tg.at[t], 15, 15, partner)
     send(ybuf.at[other], tg.at[ty], 16, 16, partner)
 
-    arrive(frame.at[pl.ds(STRIP, STRIP)], 0)
-    arrive(frame.at[pl.ds(2 * STRIP, BLK)], 1)
+    told(1)
+    tell(2)
+    arrive(frame.at[pl.ds(STRIP, BLK)], 35)
+
+    @pl.when(last)
+    def _():
+        inner[1].start()
+
+    arrive(frame.at[pl.ds(STRIP + BLK, BLK)], 36)
+    arrive(frame.at[pl.ds(2 * STRIP, BLK)], 37)
     keep1 = jnp.where(t < 15, 1.0, 0.0).astype(F32)
     keep2 = jnp.where(t < 14, 1.0, 0.0).astype(F32)
     row = lax.broadcasted_iota(jnp.int32, (TS, 2 * BLK), 0)
@@ -216,12 +250,15 @@
     fill.wait()
     send(tg, tr, 18, 18, partner)
 
+    told(2)
+    tell(3)
+
     arrive(precv, 17)
     for i in range(2):
         pown[i, 0:KH, :] = pown[i, 0:KH, :] + precv[i].astype(F32)
         for n in range(CHIPS):
             comb[n, i] = pown[i, n * KC : (n + 1) * KC, :].astype(BF)
-    for d in range(1, CHIPS):
+    for d in FAR_FIRST:
         to = lax.rem(j + d, CHIPS)
         send(comb.at[to], rsb.at[d - 1], 18 + d, 18 + d, near(to * 2 + c))
 
@@ -244,9 +281,12 @@
     for d in range(1, CHIPS):
         total = total + rsb[d - 1].astype(F32)
     gall[c, j] = total.astype(BF)
-    for d in range(1, CHIPS):
+    for d in FAR_FIRST:
         to = lax.rem(j + d, CHIPS)
         send(gall.at[c, j], gall.at[c, j], 25 + d, 25 + d, near(to * 2 + c))
+    send(gall.at[c, j], gall.at[c, j], 38, 38, partner)
+    told(3)
+    tell(4)
 
     for n in range(2):
         for q in range(NQ):
@@ -256,10 +296,12 @@
             hsp[n, q, :, 0:BLK] = real
             hsp[n, q, :, BLK:] = imag
 
-    for d in range(1, CHIPS):
-        arrive(gall.at[c, lax.rem(j + CHIPS - d, CHIPS)], 25 + d)
-    send(gall.at[c], gall.at[c], 33, 33, partner)
-    arrive(gall.at[other], 33)
+    for d in FAR_FIRST[::-1]:
+        src = lax.rem(j + CHIPS - d, CHIPS)
+        arrive(gall.at[c, src], 25 + d)
+        send(gall.at[c, src], gall.at[c, src], 38 + d, 38 + d, partner)
+    for d in range(CHIPS):
+        arrive(gall.at[other, lax.rem(j + CHIPS - d, CHIPS)], 38 + d)
 
     def power(q):
         return jnp.concatenate([gall[q // 2, n, q % 2].astype(F32) for n in range(CHIPS)], 0)
@@ -299,8 +341,8 @@
         to = lax.rem(o + d, 32)
         return remote(sbuf.at[to], rbuf.at[o], asem.at[d], bsem.at[d], (t, to))
 
-    def a2a_start(d, carry):
-        a2a(d).start()
+    def a2a_start(i, carry):
+        a2a(16 + (i + 1) // 2 * (1 - 2 * (i % 2))).start()
         return carry
 
     def a2a_wait(d, carry):
@@ -312,11 +354,18 @@
         a2a(d).wait_send()
         return carry
 
-    lax.fori_loop(1, 32, a2a_start, 0)
+    told(4)
+    lax.fori_loop(0, 31, a2a_start, 0)
     keep_own = pltpu.make_async_copy(sbuf.at[o], rbuf.at[o], lsem.at[7])
     keep_own.start()
     for copy in started:
         copy.wait_send()
+
+    @pl.when(last)
+    def _():
+        for copy in inner:
+            copy.wait_send()
+
     keep_own.wait()
     lax.fori_loop(1, 32, a2a_wait, 0)
     best = jnp.full((8, BLK), -jnp.inf, F32)
@@ -330,8 +379,8 @@
         second = second + (a * a + b * b)
     mean = first / 64.0
     spread = second / 64.0 - mean * mean
-    top_o[...] = best
-    z_o[...] = (best - mean) / jnp.sqrt(spread + 1e-05)
+    res_o[0:8] = best
+    res_o[8:16] = (best - mean) / jnp.sqrt(spread + 1e-05)
     lax.fori_loop(1, 32, a2a_sent, 0)
 
 
@@ -341,11 +390,11 @@
     vmem = pl.BlockSpec(memory_space=pltpu.VMEM)
     smem = pl.BlockSpec(memory_space=pltpu.SMEM)
     v = pltpu.VMEM
-    return pl.pallas_call(
+    both = pl.pallas_call(
         kernel,
-        out_shape=(jax.ShapeDtypeStruct((8, OUTC), F32),) * 2,
+        out_shape=jax.ShapeDtypeStruct((16, OUTC), F32),
         in_specs=[hbm, hbm, smem, smem, hbm, hbm, hbm, hbm, vmem],
-        out_specs=(vmem, vmem),
+        out_specs=vmem,
         scratch_shapes=[
             v((2 * KH, LROW), BF),
             v((NQ, LCOL, 2 * BLK), BF),
@@ -373,14 +422,16 @@
             v((32, 16, BLK), BF),
             v((32, 16, BLK), BF),
             pltpu.SemaphoreType.DMA((8,)),
-            pltpu.SemaphoreType.DMA((34,)),
-            pltpu.SemaphoreType.DMA((34,)),
+            pltpu.SemaphoreType.DMA((46,)),
+            pltpu.SemaphoreType.DMA((46,)),
             pltpu.SemaphoreType.DMA((32,)),
             pltpu.SemaphoreType.DMA((32,)),
+            pltpu.SemaphoreType.REGULAR((4,)),
         ],
         compiler_params=pltpu.CompilerParams(collective_id=0, has_side_effects=True),
         name="match",
     )(micrograph, templates, defocus, group_of_tile, rows, col, back, out, col_sum)
+    return both[0:8], both[8:16]
 
 
 def solution(mesh):

time: 58.7 us -> 53.8 us (0.917)
  Pallas kernels: 55.3 us -> 51 us
    pallas_call x1, Pallas kernels: 55.3 us -> 51 us  [local(): pl.pallas_call(kernel, out_shape=jax.ShapeDtypeStruct((16, OUTC), F32), i...]
    unnamed x4 -> x0, local copies, waits for them, and re-layouts: 1.86 us -> none
    slice x0 -> x1, local copies, waits for them, and re-layouts: none -> 1.28 us  [local(): return (both[0:8], both[8:16])]
where the time goes in v1:
time: 53.8 us; the launch traced here: 53.6 us
  Pallas kernels  51 us (95%)
  local copies, waits for them, and re-layouts  1.28 us (2%)
  between operations  1.28 us (2%)
    pallas_call x1, Pallas kernels, local(): pl.pallas_call(kernel, out_shape=jax.ShapeDtypeStruct((16, OUTC), F32), i...  51 us
    slice x1, local copies, waits for them, and re-layouts, local(): return (both[0:8], both[8:16])  1.28 us

profile of v1, /device:TPU:1, one launch (start us, length us, event | category | flops | bytes accessed | tf_op | source)
XLA Modules:
  0.0 53.6 jit_solution(13683688063797771017)
XLA Ops:
  1.3 51.0 %match.1 = f32[16,128]{1,0:T(8,128)} custom-call(bf16[256,512]{1,0:T(8,128)(2,1)} %mic.1, bf16[2,24,384]{2,1,0:T(8,128)(2,1)} %tpl.1, f32[4]{0:T(128)} %defo.1, s32[1]{0:T(128)S(6)} %copy.11.group, bf16[672,640]{1,0:T(8,128)(2,1)} %constant.10.clone.rows_h, bf16[4,512,256]{2,1,0:T(8,128)(2,1)} %constant.11.clone.col_h, ...), custom_call_target="tpu_custom_call" | custom-call | tf_op jit(solution)/shard_map/match/pallas_call | solution.py:393
  52.3 1.3 %fusion = (f32[8,128]{1,0:T(8,128)}, f32[8,128]{1,0:T(8,128)}) fusion(f32[16,128]{1,0:T(8,128)} %match.1), kind=kLoop, calls=%fused_computation | loop fusion | bytes 16384 | tf_op jit(solution)/shard_map/slice | solution.py:434

commit v2 on v1

--- a/solution.py
+++ b/solution.py
@@ -70,10 +70,10 @@
 
 
 def kernel(
-    mic, tpl, defo, group, rows_h, col_h, back_h, out_h, col_sum,
+    mic, tpl, defo_h, group_h, rows_h, col_h, back_h, out_h, sum_h,
     res_o,
-    rows, col, back, outt, frame, cspec, spec, ybuf, tg, tr, tf, tspec, hsp,
-    psend, pown, precv, comb, rsb, gall, ctf_s, ctf_c, qb, ys, sbuf, rbuf,
+    rows, col, back, outt, defo, group, col_sum, frame, begun, spec, ybuf, tg, tr, tf, tspec, hsp,
+    psend, precv, comb, rsb, gall, ctf_s, ctf_c, qb, ys, sbuf, rbuf,
     lsem, ssem, rsem, asem, bsem, esem,
 ):
     t, o = lax.axis_index("tile"), lax.axis_index("orient")
@@ -95,9 +95,10 @@
         pltpu.make_async_copy(back_h, back, lsem.at[3]),
         pltpu.make_async_copy(out_h, outt, lsem.at[4]),
         pltpu.make_async_copy(tpl.at[c], tg.at[t], lsem.at[5]),
+        pltpu.make_async_copy(defo_h, defo, lsem.at[9]),
+        pltpu.make_async_copy(group_h, group, lsem.at[10]),
+        pltpu.make_async_copy(sum_h, col_sum, lsem.at[11]),
     ]
-    for copy in loads:
-        copy.start()
 
     barrier = pltpu.get_barrier_semaphore()
 
@@ -121,6 +122,8 @@
     for d in range(1, CHIPS):
         greet(near(lax.rem(j + d, CHIPS) * 2 + c))
 
+    for copy in loads:
+        copy.start()
     started = []
 
     def remote(src, dst, send, recv, device):
@@ -173,11 +176,13 @@
     tell(1)
     loads[0].wait()
     loads[1].wait()
+    loads[2].wait()
     for q in range(NQ):
-        cspec[q, 0:STRIP, :] = jnp.dot(
-            frame[0:STRIP, :], col[q], preferred_element_type=F32
-        ).astype(BF)
-
+        part = jnp.dot(frame[0:STRIP, :], col[q], preferred_element_type=F32).astype(BF)
+        begun[q] = jnp.dot(rows[:, 0:STRIP], part, preferred_element_type=F32)
+
+    for n in (6, 7, 8):
+        loads[n].wait()
     chosen = group[0]
     depth = jnp.float32(0.0)
     for g in range(4):
@@ -220,23 +225,34 @@
     keep2 = jnp.where(t < 14, 1.0, 0.0).astype(F32)
     row = lax.broadcasted_iota(jnp.int32, (TS, 2 * BLK), 0)
     keep = jnp.where(row < STRIP, keep1, keep2)
-    for q in range(NQ):
+
+    def spectrum(q):
         part = jnp.dot(frame[STRIP:LROW, :], col[q], preferred_element_type=F32)
-        cspec[q, STRIP:LROW, :] = (part * keep).astype(BF)
-    loads[2].wait()
-
-    def spectrum(q):
-        real, imag = combine(jnp.dot(rows[...], cspec[q], preferred_element_type=F32))
+        part = (part * keep).astype(BF)
+        real, imag = combine(
+            begun[q] + jnp.dot(rows[:, STRIP:LROW], part, preferred_element_type=F32)
+        )
         spec[q, :, 0:BLK] = real
         spec[q, :, BLK:] = imag
         return real * real + imag * imag
 
     for i in range(2):
         psend[i] = spectrum(2 * other + i).astype(BF)
-    send(psend, precv, 17, 17, partner)
+        send(psend.at[i], precv.at[i], 17 + i, 17 + i, partner)
+
     for i in range(2):
-        pown[i, 0:KH, :] = spectrum(2 * c + i)
-        pown[i, KH:KP, :] = jnp.zeros((KP - KH, BLK), F32)
+        own = spectrum(2 * c + i)
+        arrive(precv.at[i], 17 + i)
+        own = own + precv[i].astype(F32)
+        for n in range(CHIPS - 1):
+            comb[i, n] = own[n * KC : (n + 1) * KC, :].astype(BF)
+        comb[i, CHIPS - 1] = jnp.zeros((KC, BLK), BF)
+        for d in FAR_FIRST:
+            to = lax.rem(j + d, CHIPS)
+            at = 39 + 7 * i + d
+            send(comb.at[i, to], rsb.at[i, d - 1], at, at, near(to * 2 + c))
+    told(2)
+    tell(3)
 
     for dx in (1, 2, 3):
         xs = lax.rem(x + 4 - dx, 4)
@@ -248,22 +264,11 @@
     arrive(tg.at[x * 4 + (1 - yh) * 2 + other], 16)
     loads[5].wait()
     fill.wait()
-    send(tg, tr, 18, 18, partner)
-
-    told(2)
-    tell(3)
-
-    arrive(precv, 17)
-    for i in range(2):
-        pown[i, 0:KH, :] = pown[i, 0:KH, :] + precv[i].astype(F32)
-        for n in range(CHIPS):
-            comb[n, i] = pown[i, n * KC : (n + 1) * KC, :].astype(BF)
-    for d in FAR_FIRST:
-        to = lax.rem(j + d, CHIPS)
-        send(comb.at[to], rsb.at[d - 1], 18 + d, 18 + d, near(to * 2 + c))
-
-    arrive(tr, 18)
+    send(tg, tr, 19, 19, partner)
+
     for n, held in enumerate((tg, tr)):
+        if n == 1:
+            arrive(tr, 19)
         for s in range(16):
             tf[s * 24 : (s + 1) * 24, :] = held[s].astype(F32)
         values = tf[...]
@@ -275,16 +280,18 @@
             part = jnp.dot(rounded, col[q, 0:TS, :], preferred_element_type=F32)
             tspec[n, q] = ((part - mean * col_sum[q]) * inverse).astype(BF)
 
-    for d in range(1, CHIPS):
-        arrive(rsb.at[d - 1], 18 + d)
-    total = comb[j].astype(F32)
-    for d in range(1, CHIPS):
-        total = total + rsb[d - 1].astype(F32)
-    gall[c, j] = total.astype(BF)
-    for d in FAR_FIRST:
-        to = lax.rem(j + d, CHIPS)
-        send(gall.at[c, j], gall.at[c, j], 25 + d, 25 + d, near(to * 2 + c))
-    send(gall.at[c, j], gall.at[c, j], 38, 38, partner)
+    for i in range(2):
+        total = comb[i, j].astype(F32)
+        for d in range(1, CHIPS):
+            arrive(rsb.at[i, d - 1], 39 + 7 * i + d)
+            total = total + rsb[i, d - 1].astype(F32)
+        gall[c, i, j] = total.astype(BF)
+        mine = gall.at[c, i, j]
+        for d in FAR_FIRST:
+            to = lax.rem(j + d, CHIPS)
+            at = 53 + 7 * i + d
+            send(mine, mine, at, at, near(to * 2 + c))
+        send(mine, mine, 68 + 8 * i, 68 + 8 * i, partner)
     told(3)
     tell(4)
 
@@ -296,15 +303,17 @@
             hsp[n, q, :, 0:BLK] = real
             hsp[n, q, :, BLK:] = imag
 
-    for d in FAR_FIRST[::-1]:
-        src = lax.rem(j + CHIPS - d, CHIPS)
-        arrive(gall.at[c, src], 25 + d)
-        send(gall.at[c, src], gall.at[c, src], 38 + d, 38 + d, partner)
-    for d in range(CHIPS):
-        arrive(gall.at[other, lax.rem(j + CHIPS - d, CHIPS)], 38 + d)
+    for i in range(2):
+        for d in FAR_FIRST[::-1]:
+            piece = gall.at[c, i, lax.rem(j + CHIPS - d, CHIPS)]
+            arrive(piece, 53 + 7 * i + d)
+            send(piece, piece, 68 + 8 * i + d, 68 + 8 * i + d, partner)
+    for i in range(2):
+        for d in range(CHIPS):
+            arrive(gall.at[other, i, lax.rem(j + CHIPS - d, CHIPS)], 68 + 8 * i + d)
 
     def power(q):
-        return jnp.concatenate([gall[q // 2, n, q % 2].astype(F32) for n in range(CHIPS)], 0)
+        return jnp.concatenate([gall[q // 2, q % 2, n].astype(F32) for n in range(CHIPS)], 0)
 
     k = lax.broadcasted_iota(jnp.int32, (KP, BLK), 0)
     weight = jnp.where(k < LROW // 2, 2.0, 1.0) * jnp.where(k <= LROW // 2, 1.0, 0.0)
@@ -319,31 +328,37 @@
         phase = depth * (lane * lane)
         factor = -(ctf_s[...] * jnp.cos(phase) + ctf_c[...] * jnp.sin(phase))
         factor = factor * lax.rsqrt(power(q)[0:KH] / 16.0 + average)
-        real, imag = spec[q, :, 0:BLK] * factor, spec[q, :, BLK:] * factor
-        for n in range(2):
-            h_re, h_im = hsp[n, q, :, 0:BLK], hsp[n, q, :, BLK:]
-            qb[n * KH : (n + 1) * KH, q * 256 : q * 256 + BLK] = (real * h_re + imag * h_im).astype(BF)
-            qb[n * KH : (n + 1) * KH, q * 256 + BLK : (q + 1) * 256] = (imag * h_re - real * h_im).astype(BF)
+        spec[q, :, 0:BLK] = spec[q, :, 0:BLK] * factor
+        spec[q, :, BLK:] = spec[q, :, BLK:] * factor
     loads[3].wait()
     loads[4].wait()
+    told(4)
+
+    def a2a(d):
+        to = lax.rem(o + d, 32)
+        return remote(sbuf.at[to], rbuf.at[o], asem.at[d], bsem.at[d], (t, to))
+
     for n in range(2):
-        y = jnp.dot(
-            qb[n * KH : (n + 1) * KH, :], back[...], preferred_element_type=F32
-        ).astype(BF)
+        for q in range(NQ):
+            real, imag = spec[q, :, 0:BLK], spec[q, :, BLK:]
+            h_re, h_im = hsp[n, q, :, 0:BLK], hsp[n, q, :, BLK:]
+            qb[n, :, q * 256 : q * 256 + BLK] = (real * h_re + imag * h_im).astype(BF)
+            qb[n, :, q * 256 + BLK : (q + 1) * 256] = (imag * h_re - real * h_im).astype(BF)
+        y = jnp.dot(qb[n], back[...], preferred_element_type=F32).astype(BF)
         ys[0:KH, n * BLK : (n + 1) * BLK] = y[:, 0:BLK]
         ys[KH:, n * BLK : (n + 1) * BLK] = y[:, BLK:]
     score = jnp.dot(outt[...], ys[...], preferred_element_type=F32)
-    for n in range(32):
-        block = score[n * 8 : (n + 1) * 8, :]
-        sbuf[n] = jnp.concatenate([block[:, 0:BLK], block[:, BLK:]], 0).astype(BF)
-
-    def a2a(d):
-        to = lax.rem(o + d, 32)
-        return remote(sbuf.at[to], rbuf.at[o], asem.at[d], bsem.at[d], (t, to))
+    for r in range(32):
+        block = score[r * 8 : (r + 1) * 8, :]
+        sbuf[r] = jnp.concatenate([block[:, 0:BLK], block[:, BLK:]], 0).astype(BF)
 
     def a2a_start(i, carry):
         a2a(16 + (i + 1) // 2 * (1 - 2 * (i % 2))).start()
         return carry
+
+    lax.fori_loop(0, 31, a2a_start, 0)
+    own_rows = pltpu.make_async_copy(sbuf.at[o], rbuf.at[o], lsem.at[7])
+    own_rows.start()
 
     def a2a_wait(d, carry):
         src = lax.rem(o + 32 - d, 32)
@@ -354,10 +369,6 @@
         a2a(d).wait_send()
         return carry
 
-    told(4)
-    lax.fori_loop(0, 31, a2a_start, 0)
-    keep_own = pltpu.make_async_copy(sbuf.at[o], rbuf.at[o], lsem.at[7])
-    keep_own.start()
     for copy in started:
         copy.wait_send()
 
@@ -366,13 +377,13 @@
         for copy in inner:
             copy.wait_send()
 
-    keep_own.wait()
+    own_rows.wait()
     lax.fori_loop(1, 32, a2a_wait, 0)
     best = jnp.full((8, BLK), -jnp.inf, F32)
     first = jnp.zeros((8, BLK), F32)
     second = jnp.zeros((8, BLK), F32)
-    for n in range(32):
-        pair = rbuf[n].astype(F32)
+    for r in range(32):
+        pair = rbuf[r].astype(F32)
         a, b = pair[0:8], pair[8:16]
         best = jnp.maximum(best, jnp.maximum(a, b))
         first = first + (a + b)
@@ -386,22 +397,24 @@
 
 def local(consts, micrograph, templates, defocus, group_of_tile):
     rows, col, back, out, col_sum = consts
-    hbm = pl.BlockSpec(memory_space=pl.ANY)
+    hbm = pl.BlockSpec(memory_space=pltpu.HBM)
     vmem = pl.BlockSpec(memory_space=pltpu.VMEM)
-    smem = pl.BlockSpec(memory_space=pltpu.SMEM)
     v = pltpu.VMEM
     both = pl.pallas_call(
         kernel,
-        out_shape=jax.ShapeDtypeStruct((16, OUTC), F32),
-        in_specs=[hbm, hbm, smem, smem, hbm, hbm, hbm, hbm, vmem],
+        out_shape=pltpu.VMEM((16, OUTC), F32),
+        in_specs=[hbm] * 9,
         out_specs=vmem,
         scratch_shapes=[
             v((2 * KH, LROW), BF),
             v((NQ, LCOL, 2 * BLK), BF),
             v((2 * LCOL, 2 * OUTC), BF),
             v((STRIP, 2 * KH), BF),
+            pltpu.SMEM((4,), F32),
+            pltpu.SMEM((1,), jnp.int32),
+            v((NQ, 1, 2 * BLK), F32),
             v((LROW, LCOL), BF),
-            v((NQ, LROW, 2 * BLK), BF),
+            v((NQ, 2 * KH, 2 * BLK), F32),
             v((NQ, KH, 2 * BLK), F32),
             v((2, 24, TS), BF),
             v((16, 24, TS), BF),
@@ -410,20 +423,19 @@
             v((2, NQ, TS, 2 * BLK), BF),
             v((2, NQ, KH, 2 * BLK), F32),
             v((2, KH, BLK), BF),
-            v((2, KP, BLK), F32),
             v((2, KH, BLK), BF),
-            v((CHIPS, 2, KC, BLK), BF),
-            v((CHIPS - 1, 2, KC, BLK), BF),
-            v((2, CHIPS, 2, KC, BLK), BF),
+            v((2, CHIPS, KC, BLK), BF),
+            v((2, CHIPS - 1, KC, BLK), BF),
+            v((2, 2, CHIPS, KC, BLK), BF),
             v((KH, BLK), F32),
             v((KH, BLK), F32),
-            v((2 * KH, 2 * LCOL), BF),
+            v((2, KH, 2 * LCOL), BF),
             v((2 * KH, 2 * BLK), BF),
             v((32, 16, BLK), BF),
             v((32, 16, BLK), BF),
-            pltpu.SemaphoreType.DMA((8,)),
-            pltpu.SemaphoreType.DMA((46,)),
-            pltpu.SemaphoreType.DMA((46,)),
+            pltpu.SemaphoreType.DMA((12,)),
+            pltpu.SemaphoreType.DMA((84,)),
+            pltpu.SemaphoreType.DMA((84,)),
             pltpu.SemaphoreType.DMA((32,)),
             pltpu.SemaphoreType.DMA((32,)),
             pltpu.SemaphoreType.REGULAR((4,)),

time: 53.8 us -> 51 us (0.948)
  Pallas kernels: 51 us -> 48.7 us
  local copies, waits for them, and re-layouts: 1.28 us -> 0.6 us
    pallas_call x1, Pallas kernels: 51 us -> 48.7 us  [local(): pl.pallas_call(kernel, out_shape=pltpu.VMEM((16, OUTC), F32), in_specs=[h...]
    slice x1, local copies, waits for them, and re-layouts: 1.28 us -> 0.6 us  [local(): return (both[0:8], both[8:16])]
where the time goes in v2:
time: 51 us; the launch traced here: 50.6 us
  Pallas kernels  48.7 us (95%)
  between operations  1.28 us (3%)
  local copies, waits for them, and re-layouts  0.6 us (1%)
    pallas_call x1, Pallas kernels, local(): pl.pallas_call(kernel, out_shape=pltpu.VMEM((16, OUTC), F32), in_specs=[h...  48.7 us

profile of v2, /device:TPU:1, one launch (start us, length us, event | category | flops | bytes accessed | tf_op | source)
XLA Modules:
  0.0 50.6 jit_solution(8598004004866610483)
XLA Ops:
  1.3 48.7 %match.1 = f32[16,128]{1,0:T(8,128)S(1)} custom-call(bf16[256,512]{1,0:T(8,128)(2,1)} %mic.1, bf16[2,24,384]{2,1,0:T(8,128)(2,1)} %tpl.1, f32[4]{0:T(128)} %defo_h.1, s32[1]{0:T(128)S(6)} %copy.11.group_h, bf16[672,640]{1,0:T(8,128)(2,1)} %constant.10.clone.rows_h, bf16[4,512,256]{2,1,0:T(8,128)(2,1)} %constant.11.clone.col_h, ...), custom_call_target="tpu_custom_call" | custom-call | tf_op jit(solution)/shard_map/match/pallas_call | solution.py:403
  50.0 0.6 %fusion = (f32[8,128]{1,0:T(8,128)}, f32[8,128]{1,0:T(8,128)}) fusion(f32[16,128]{1,0:T(8,128)S(1)} %match.1), kind=kLoop, calls=%fused_computation | loop fusion | bytes 16384 | tf_op jit(solution)/shard_map/slice | solution.py:446

commit v3 on v2

--- a/solution.py
+++ b/solution.py
@@ -352,22 +352,14 @@
         block = score[r * 8 : (r + 1) * 8, :]
         sbuf[r] = jnp.concatenate([block[:, 0:BLK], block[:, BLK:]], 0).astype(BF)
 
-    def a2a_start(i, carry):
+    for i in range(31):
         a2a(16 + (i + 1) // 2 * (1 - 2 * (i % 2))).start()
-        return carry
-
-    lax.fori_loop(0, 31, a2a_start, 0)
     own_rows = pltpu.make_async_copy(sbuf.at[o], rbuf.at[o], lsem.at[7])
     own_rows.start()
 
-    def a2a_wait(d, carry):
+    def a2a_wait(d):
         src = lax.rem(o + 32 - d, 32)
         remote(rbuf.at[src], rbuf.at[src], asem.at[d], bsem.at[d], partner).wait_recv()
-        return carry
-
-    def a2a_sent(d, carry):
-        a2a(d).wait_send()
-        return carry
 
     for copy in started:
         copy.wait_send()
@@ -378,7 +370,8 @@
             copy.wait_send()
 
     own_rows.wait()
-    lax.fori_loop(1, 32, a2a_wait, 0)
+    for d in range(1, 32):
+        a2a_wait(d)
     best = jnp.full((8, BLK), -jnp.inf, F32)
     first = jnp.zeros((8, BLK), F32)
     second = jnp.zeros((8, BLK), F32)
@@ -392,7 +385,8 @@
     spread = second / 64.0 - mean * mean
     res_o[0:8] = best
     res_o[8:16] = (best - mean) / jnp.sqrt(spread + 1e-05)
-    lax.fori_loop(1, 32, a2a_sent, 0)
+    for d in range(1, 32):
+        a2a(d).wait_send()
 
 
 def local(consts, micrograph, templates, defocus, group_of_tile):

time: 51 us -> 50.9 us (level)
  no operation moved by 1% of the time
where the time goes in v3:
time: 50.9 us; the launch traced here: 50.3 us
  Pallas kernels  48.4 us (95%)
  between operations  1.28 us (3%)
  local copies, waits for them, and re-layouts  0.6 us (1%)
    pallas_call x1, Pallas kernels, local(): pl.pallas_call(kernel, out_shape=pltpu.VMEM((16, OUTC), F32), in_specs=[h...  48.4 us

profile of v3, /device:TPU:1, one launch (start us, length us, event | category | flops | bytes accessed | tf_op | source)
XLA Modules:
  0.0 50.3 jit_solution(7702468949424388685)
XLA Ops:
  1.3 48.4 %match.1 = f32[16,128]{1,0:T(8,128)S(1)} custom-call(bf16[256,512]{1,0:T(8,128)(2,1)} %mic.1, bf16[2,24,384]{2,1,0:T(8,128)(2,1)} %tpl.1, f32[4]{0:T(128)} %defo_h.1, s32[1]{0:T(128)S(6)} %copy.11.group_h, bf16[672,640]{1,0:T(8,128)(2,1)} %constant.10.clone.rows_h, bf16[4,512,256]{2,1,0:T(8,128)(2,1)} %constant.11.clone.col_h, ...), custom_call_target="tpu_custom_call" | custom-call | tf_op jit(solution)/shard_map/match/pallas_call | solution.py:397
  49.7 0.6 %fusion = (f32[8,128]{1,0:T(8,128)}, f32[8,128]{1,0:T(8,128)}) fusion(f32[16,128]{1,0:T(8,128)S(1)} %match.1), kind=kLoop, calls=%fused_computation | loop fusion | bytes 16384 | tf_op jit(solution)/shard_map/slice | solution.py:440

commit v4 on v3

--- a/solution.py
+++ b/solution.py
@@ -280,7 +280,7 @@
             part = jnp.dot(rounded, col[q, 0:TS, :], preferred_element_type=F32)
             tspec[n, q] = ((part - mean * col_sum[q]) * inverse).astype(BF)
 
-    for i in range(2):
+        i = n
         total = comb[i, j].astype(F32)
         for d in range(1, CHIPS):
             arrive(rsb.at[i, d - 1], 39 + 7 * i + d)

time: 50.9 us -> 50.6 us (level)
  no operation moved by 1% of the time
where the time goes in v4:
time: 50.6 us; the launch traced here: 50.3 us
  Pallas kernels  48.4 us (96%)
  between operations  1.28 us (3%)
  local copies, waits for them, and re-layouts  0.6 us (1%)
    pallas_call x1, Pallas kernels, local(): pl.pallas_call(kernel, out_shape=pltpu.VMEM((16, OUTC), F32), in_specs=[h...  48.4 us

profile of v4, /device:TPU:1, one launch (start us, length us, event | category | flops | bytes accessed | tf_op | source)
XLA Modules:
  0.0 50.3 jit_solution(12249193910203283298)
XLA Ops:
  1.3 48.4 %match.1 = f32[16,128]{1,0:T(8,128)S(1)} custom-call(bf16[256,512]{1,0:T(8,128)(2,1)} %mic.1, bf16[2,24,384]{2,1,0:T(8,128)(2,1)} %tpl.1, f32[4]{0:T(128)} %defo_h.1, s32[1]{0:T(128)S(6)} %copy.11.group_h, bf16[672,640]{1,0:T(8,128)(2,1)} %constant.10.clone.rows_h, bf16[4,512,256]{2,1,0:T(8,128)(2,1)} %constant.11.clone.col_h, ...), custom_call_target="tpu_custom_call" | custom-call | tf_op jit(solution)/shard_map/match/pallas_call | solution.py:397
  49.7 0.6 %fusion = (f32[8,128]{1,0:T(8,128)}, f32[8,128]{1,0:T(8,128)}) fusion(f32[16,128]{1,0:T(8,128)S(1)} %match.1), kind=kLoop, calls=%fused_computation | loop fusion | bytes 16384 | tf_op jit(solution)/shard_map/slice | solution.py:440
